TPU v7x, 32 devices: a whole 2x2x4 slice. The times are simulated.
32 devices in a mesh: row: 8 (over y, x, core), col: 4 (over z).
Axes of the slice: x: 2, y: 2, z: 4, core: 2. Of those that a mesh axis runs over, the one named last changes fastest.
Arguments:
- skew_matrix: float32 [16384, 16384], P('row', 'col'), may hold values from -80 to 80, as said below
- first_reflector: float32 [16384, 128], P('row'), may hold values from -0.05625 to 0.05625
- first_factor: float32 [128, 128], replicated, may hold values from -0.6 to 1.5, as said below
- second_reflector: float32 [16384, 128], P('row'), may hold values from -0.05625 to 0.05625
- second_factor: float32 [128, 128], replicated, may hold values from -0.6 to 1.5, as said below
- vectors: float32 [16384, 4096], P('row', 'col'), may hold values from -6 to 6
Outputs:
- updated_matrix: float32 [16384, 16384], P('row', 'col')
- back_vectors: float32 [16384, 4096], P('row', 'col')
Inputs may be any that keep to these rules, and one draw needn't show every extreme that they name: skew_matrix is skew-symmetric: entry (i, j) equals minus entry (j, i) exactly. first_factor is upper triangular with a positive diagonal. second_factor is upper triangular with a positive diagonal.
All inputs are finite; a program needn't handle non-finite values.
Results may differ from a plain program's by a relative error of at most 0.000059.
Values sent between devices are 32-bit elements; how exact they have to be, the bound alone decides.
A program may use at most 192 MiB of HBM per device.

v0:
```python
import jax
import jax.numpy as jnp
from jax import lax
from jax.sharding import PartitionSpec as P


def multiply(left, right):
    return jnp.dot(left, right, precision=lax.Precision.HIGHEST, preferred_element_type=jnp.float32)


def inner_rows(left, right):
    return lax.dot_general(
        left,
        right,
        (((0,), (0,)), ((), ())),
        precision=lax.Precision.HIGHEST,
        preferred_element_type=jnp.float32,
    )


def transform(matrix, own_rows, col_rows, factor):
    partial_rows = multiply(matrix, col_rows)
    summed_rows = lax.psum(partial_rows, "col")
    partial_cols = inner_rows(matrix, own_rows)
    summed_cols = lax.psum(partial_cols, "row")
    plain_cols = -summed_cols
    gram = lax.psum(inner_rows(own_rows, summed_rows), "row")
    correction = multiply(multiply(factor.T, gram), factor)
    fixed_rows = multiply(summed_rows, factor) - 0.5 * multiply(own_rows, correction)
    fixed_cols = multiply(plain_cols, factor) - 0.5 * multiply(col_rows, correction)
    left = jnp.concatenate([own_rows, -fixed_rows], axis=1)
    right = jnp.concatenate([fixed_cols, col_rows], axis=1)
    update = lax.dot_general(
        left,
        right,
        (((1,), (1,)), ((), ())),
        precision=lax.Precision.HIGHEST,
        preferred_element_type=jnp.float32,
    )
    return matrix + update


def shards(skew_matrix, first_reflector, first_factor, second_reflector, second_factor, vectors):
    joined = jnp.concatenate([first_reflector, second_reflector], axis=1)
    correlation, projected = lax.psum(
        (inner_rows(first_reflector, second_reflector), inner_rows(joined, vectors)), "row"
    )
    top_right = -multiply(multiply(first_factor, correlation), second_factor)
    zeros_block = jnp.zeros_like(second_factor)
    compact = jnp.concatenate(
        [
            jnp.concatenate([first_factor, top_right], axis=1),
            jnp.concatenate([zeros_block, second_factor], axis=1),
        ],
        axis=0,
    )
    back_vectors = vectors - multiply(joined, multiply(compact, projected))
    cols_here = skew_matrix.shape[1]
    col_index = lax.axis_index("col")
    whole_first, whole_second = (
        lax.all_gather(first_reflector, "row", axis=0, tiled=True),
        lax.all_gather(second_reflector, "row", axis=0, tiled=True),
    )
    col_start = col_index * cols_here
    panel_first = lax.dynamic_slice_in_dim(whole_first, col_start, cols_here, 0)
    panel_second = lax.dynamic_slice_in_dim(whole_second, col_start, cols_here, 0)
    inner = transform(skew_matrix, first_reflector, panel_first, first_factor)
    updated_matrix = transform(inner, second_reflector, panel_second, second_factor)
    return (updated_matrix, back_vectors)


def solution(mesh):
    in_specs = (P("row", "col"), P("row", None), P(), P("row", None), P(), P("row", "col"))
    out_specs = (P("row", "col"), P("row", "col"))
    return jax.shard_map(shards, mesh=mesh, in_specs=in_specs, out_specs=out_specs, check_vma=False)
```

profile of v0, /device:TPU:0, one launch (start us, length us, event | category | flops | bytes accessed | tf_op | source)
XLA Modules:
  0.0 549.0 jit_solution(17140156105039725318)
XLA Ops:
  7.2 0.0 all-gather.3.cloned.1.call-start
  7.2 0.7 all-gather.3.cloned.1.call-update
  7.9 0.0 all-reduce.8.cloned.1.call-start
  7.9 58.9 %all-gather.3.cloned.1.call-done = f32[16384,128]{1,0:T(8,128)} async-done(((f32[2048,128]{1,0:T(8,128)}), f32[16384,128]{1,0:T(8,128)}) %all-gather.3.cloned.1.call-update) | async-done | bytes 8388624 | tf_op jit(solution)/shard_map/all_gather | solution.py:61
  66.9 1.7 constant_dynamic-slice_fusion.1
  68.6 0.0 copy-start.4
  68.6 1.3 copy-done.4
  69.9 41.9 %convolution_bitcast_fusion = f32[2048,128]{0,1:T(8,128)} fusion(f32[4096,128]{1,0:T(8,128)S(1)} %constant_dynamic-slice_fusion.1, f32[2048,4096]{1,0:T(8,128)} %param.6), kind=kOutput, calls=%fused_computation.13 | convolution fusion | flops 12884901888 | bytes 36700160 | tf_op jit(solution)/shard_map/dot_general | solution.py:8
  111.8 0.0 copy-start
  111.8 0.0 copy-start.1
  111.8 0.0 all-reduce.8.cloned.1.call-update
  111.8 0.0 all-gather.5.cloned.1.call-start
  111.9 0.7 all-gather.5.cloned.1.call-update
  112.6 0.0 all-reduce.14.cloned.1.call-start
  112.6 0.4 copy-done
  113.0 1.1 constant_dynamic-update-slice_fusion.1
  114.1 0.0 copy-done.1
  114.1 1.1 constant_dynamic-update-slice_fusion
  115.2 57.1 %fusion.39 = f32[4096,128]{1,0:T(8,128)} fusion(f32[2048,4096]{1,0:T(8,128)} %param.6, f32[2048,128]{1,0:T(8,128)S(1)} %copy-done), kind=kOutput, calls=%fused_computation.56 | convolution fusion | flops 12884901888 | bytes 36700160 | tf_op jit(solution)/shard_map/dot_general | solution.py:12
  172.3 0.0 all-reduce.8.cloned.1.call-done
  172.3 3.1 convolution_bitcast_fusion.2
  175.4 0.0 all-reduce.14.cloned.1.call-update
  175.4 0.0 all-reduce.10.cloned.1.call-start
  175.5 11.1 %fusion.47 = f32[256,1024]{1,0:T(8,128)} fusion(f32[2048,256]{1,0:T(8,128)} %constant_dynamic-update-slice_fusion, f32[2048,1024]{1,0:T(8,128)} %param.11), kind=kOutput, calls=%fused_computation.64 | convolution fusion | flops 6442450944 | bytes 11534336 | tf_op jit(solution)/shard_map/dot_general | solution.py:12
  186.5 2.4 fusion.45
  189.0 30.4 %all-gather.5.cloned.1.call-done = f32[16384,128]{1,0:T(8,128)} async-done(((f32[2048,128]{1,0:T(8,128)}), f32[16384,128]{1,0:T(8,128)}) %all-gather.5.cloned.1.call-update) | async-done | bytes 8388624 | tf_op jit(solution)/shard_map/all_gather | solution.py:62
  219.3 3.2 constant_dynamic-slice_fusion
  222.6 0.0 copy-done.8
  222.6 0.0 copy-done.6
  222.6 1.8 fusion.36
  224.4 60.9 %all-reduce.14.cloned.1.call-done = (f32[4096,128]{1,0:T(8,128)}, f32[128,128]{0,1:T(8,128)}) async-done(((f32[4096,128]{1,0:T(8,128)}, f32[128,128]{0,1:T(8,128)}), (f32[4096,128]{1,0:T(8,128)}, f32[128,128]{0,1:T(8,128)})) %all-reduce.14.cloned.1.call-update) | async-done | bytes 2162704 | tf_op jit(solution)/shard_map/psum | solution.py:25
  285.3 3.6 fusion.22
  288.9 0.0 copy-done.12
  288.9 0.2 fusion.37
  289.1 0.3 fusion.38
  289.4 0.0 copy-done.5
  289.4 1.9 fusion.1
  291.3 1.0 fusion.13
  292.3 0.0 copy-start.2
  292.3 33.7 %convolution_add_fusion.1 = f32[2048,4096]{1,0:T(8,128)} fusion(f32[2048,4096]{1,0:T(8,128)} %param.6, f32[4096,128]{1,0:T(8,128)S(1)} %copy-done.5, f32[4096,128]{1,0:T(8,128)S(1)} %fusion.1, f32[2048,128]{1,0:T(8,128)S(1)} %fusion.13, f32[2048,128]{1,0:T(8,128)S(1)} %copy-done), kind=kOutput, calls=%fused_computation.1 | convolution fusion | flops 25779765248 | bytes 73400320 | tf_op jit(solution)/shard_map/dot_general | solution.py:33
  325.9 0.0 copy-done.2
  325.9 30.9 %fusion.40 = f32[2048,128]{1,0:T(8,128)} fusion(f32[2048,4096]{1,0:T(8,128)} %convolution_add_fusion.1, f32[4096,128]{1,0:T(8,128)S(1)} %copy-done.2), kind=kOutput, calls=%fused_computation.57 | convolution fusion | flops 12884901888 | bytes 36700160 | tf_op jit(solution)/shard_map/dot_general | solution.py:8
  356.8 0.0 all-reduce.10.cloned.1.call-update
  356.8 0.0 all-reduce.12.cloned.1.call-start
  356.9 57.1 %fusion.44 = f32[4096,128]{1,0:T(8,128)} fusion(f32[2048,4096]{1,0:T(8,128)} %convolution_add_fusion.1, f32[2048,128]{1,0:T(8,128)S(1)} %copy-done.1), kind=kOutput, calls=%fused_computation.61 | convolution fusion | flops 12884901888 | bytes 36700160 | tf_op jit(solution)/shard_map/dot_general | solution.py:12
  414.0 0.0 all-reduce.10.cloned.1.call-done
  414.0 3.7 convolution_bitcast_fusion.1
  417.7 0.0 all-reduce.12.cloned.1.call-update
  417.7 1.2 copy-done.7
  418.9 1.0 fusion.41
  419.9 68.0 %all-reduce.12.cloned.1.call-done = (f32[4096,128]{1,0:T(8,128)}, f32[128,128]{0,1:T(8,128)}, f32[256,1024]{1,0:T(8,128)}, f32[128,128]{1,0:T(8,128)}) async-done(((f32[4096,128]{1,0:T(8,128)}, f32[128,128]{0,1:T(8,128)}, f32[256,1024]{1,0:T(8,128)}, f32[128,128]{1,0:T(8,128)}), (f32[4096,128]{1,0:T(8,128)}, f32[128,128]{0,1:T(8,128)}, f32[256,1024]{1,0:T(8,128)}, ...) | async-done | bytes 3276816 | tf_op jit(solution)/shard_map/psum | solution.py:25
  487.9 3.6 fusion.20
  491.5 0.2 fusion.42
  491.7 0.3 fusion.43
  492.0 1.9 fusion
  493.8 0.0 copy-start.11
  493.9 0.0 copy-start.10
  493.9 1.0 fusion.10
  494.9 0.3 fusion.46
  495.2 0.3 convolution_negate_fusion
  495.5 0.0 copy-done.10
  495.5 1.0 fusion.24
  496.5 12.2 %convolution_subtract_fusion = f32[2048,1024]{1,0:T(8,128)} fusion(f32[2048,1024]{1,0:T(8,128)} %param.11, f32[2048,256]{1,0:T(8,128)} %constant_dynamic-update-slice_fusion, f32[256,1024]{1,0:T(8,128)S(1)} %fusion.24), kind=kOutput, calls=%fused_computation.6 | convolution fusion | flops 6444548096 | bytes 19922944 | tf_op jit(solution)/shard_map/dot_general | solution.py:8
  508.7 33.0 %convolution_add_fusion = f32[2048,4096]{1,0:T(8,128)} fusion(f32[2048,4096]{1,0:T(8,128)} %convolution_add_fusion.1, f32[4096,128]{1,0:T(8,128)S(1)} %copy-done.3, f32[4096,128]{1,0:T(8,128)S(1)} %fusion, f32[2048,128]{1,0:T(8,128)S(1)} %fusion.10, f32[2048,128]{1,0:T(8,128)S(1)} %copy-done.1), kind=kOutput, calls=%fused_computation | convolution fusion | flops 25779765248 | bytes 73400320 | tf_op jit(solution)/shard_map/dot_general | solution.py:33
  (12 shorter events, 0.0 us)
Async XLA Ops:
  7.2 59.7 %all-gather.3.cloned.1.call-start = ((), (), s32[]{:S(2)}) async-start(), calls=%async_computation | async-start | bytes 9437184 | tf_op jit(solution)/shard_map/all_gather | solution.py:61
  7.9 164.4 %all-reduce.8.cloned.1.call-start = ((), (), s32[]{:S(2)}) async-start(), calls=%async_computation.1 | async-start | bytes 2097152 | tf_op jit(solution)/shard_map/psum | solution.py:23
  68.6 1.3 copy-start.4
  111.8 1.2 copy-start
  111.8 2.3 copy-start.1
  111.8 107.5 %all-gather.5.cloned.1.call-start = ((), (), s32[]{:S(2)}) async-start(), calls=%async_computation.2 | async-start | bytes 9437184 | tf_op jit(solution)/shard_map/all_gather | solution.py:62
  112.6 172.7 %all-reduce.14.cloned.1.call-start = ((), (), s32[]{:S(2)}) async-start(), calls=%async_computation.5 | async-start | bytes 4325376 | tf_op jit(solution)/shard_map/psum | solution.py:25
  175.4 238.6 %all-reduce.10.cloned.1.call-start = ((), (), s32[]{:S(2)}) async-start(), calls=%async_computation.3 | async-start | bytes 2097152 | tf_op jit(solution)/shard_map/psum | solution.py:23
  189.0 33.6 %copy-start.8 = (f32[128,128]{1,0:T(8,128)S(1)}, f32[128,128]{1,0:T(8,128)}, u32[]{:S(2)}) copy-start(f32[128,128]{1,0:T(8,128)} %param.8) | copy-start | bytes 196612
  219.3 3.2 copy-start.6
  285.3 3.6 copy-start.12
  285.3 4.1 copy-start.5
  292.3 33.7 %copy-start.2 = (f32[4096,128]{1,0:T(8,128)S(1)}, f32[4096,128]{1,0:T(8,128)}, u32[]{:S(2)}) copy-start(f32[4096,128]{1,0:T(8,128)} %constant_dynamic-slice_fusion) | copy-start | bytes 6291460
  356.8 131.0 %all-reduce.12.cloned.1.call-start = ((), (), s32[]{:S(2)}) async-start(), calls=%async_computation.4 | async-start | bytes 6553600 | tf_op jit(solution)/shard_map/psum | solution.py:25
  417.7 1.2 copy-start.7
  417.7 1.2 copy-start.9
  487.9 3.6 copy-start.13
  487.9 4.1 copy-start.3
  493.8 1.0 copy-start.11
  493.9 1.6 copy-start.10
Sparse Core Ops, SparseCore 0:
  9.9 56.9 all-gather.2
  112.0 51.8 all-reduce.7
  165.8 53.5 all-gather.4
  223.1 62.1 all-reduce.13
  357.0 51.0 all-reduce.9
  417.8 70.0 all-reduce.11
where the time goes:
time: 559 us; the launch traced here: 549 us
  matrix products  304 us (54%)
  waiting for transfers between devices  220 us (39%)
  between operations  14.8 us (3%)
  local copies, waits for them, and re-layouts  10 us (2%)
    dot_general x6, matrix products, inner_rows(): lax.dot_general(left, right, (((0,), (0,)), ((), ())), precision=lax.Prec...  134 us
    psum x2, waiting for transfers between devices, transform(): summed_cols = lax.psum(partial_cols, 'row')  129 us
    dot_general x18, matrix products, multiply(): jnp.dot(left, right, precision=lax.Precision.HIGHEST, preferred_element_t...  103 us
    dot_general x2, matrix products, transform(): lax.dot_general(left, right, (((1,), (1,)), ((), ())), precision=lax.Prec...  66.7 us
    all_gather x1, waiting for transfers between devices, shards(): lax.all_gather(first_reflector, 'row', axis=0, tiled=True)  58.9 us
    all_gather x1, waiting for transfers between devices, shards(): lax.all_gather(second_reflector, 'row', axis=0, tiled=True)  30.4 us
  transfers between devices with their start and end apart: 6, of which 4 were waited for; matrix products, arithmetic and copies ran while one was open for 25% of the time, Pallas kernels for 0%

commit v1 on v0

v1 whole, which is shorter than its diff:
```python
import jax
import jax.numpy as jnp
from jax import lax
from jax.sharding import PartitionSpec as P

HIGH = lax.Precision.HIGH
FULL = lax.Precision.HIGHEST


def dot(left, right, dims, precision=HIGH):
    return lax.dot_general(
        left, right, (dims, ((), ())), precision=precision, preferred_element_type=jnp.float32
    )


NN = ((1,), (0,))
TN = ((0,), (0,))
NT = ((1,), (1,))


def panel_of(block, rows, cols):
    share = rows // cols
    length = block.shape[0]
    col = lax.axis_index("col")
    row = lax.axis_index("row")
    if rows % cols or cols & (cols - 1) or cols < 2 or share != 2:
        whole = lax.all_gather(block, "row", axis=0, tiled=True)
        width = length * rows // cols
        return lax.dynamic_slice_in_dim(whole, col * width, width, 0)
    bits = []
    bit = 1
    while bit < cols:
        bits.append(bit)
        bit *= 2
    have = (row // share) == col
    pieces = []
    half = length // 2
    for turn in range(2):
        order = bits[turn:] + bits[:turn]
        part = jnp.where(have, block[turn * half : (turn + 1) * half], 0.0)
        reached = [0]
        for bit in order:
            pairs = []
            for c in range(cols):
                for offset in reached:
                    k = c ^ offset
                    for j in range(share):
                        pairs.append(((k * share + j) * cols + c, ((k ^ bit) * share + j) * cols + c))
            part = part + lax.ppermute(part, ("row", "col"), pairs)
            reached = reached + [offset ^ bit for offset in reached]
        swap = [(r, r ^ 1) for r in range(rows)]
        other = lax.ppermute(part, "row", swap)
        pieces.append((part, other))
    first = jnp.concatenate([pieces[0][0], pieces[1][0]], axis=0)
    second = jnp.concatenate([pieces[0][1], pieces[1][1]], axis=0)
    even = (row % 2) == 0
    return jnp.concatenate([jnp.where(even, first, second), jnp.where(even, second, first)], axis=0)


def solution(mesh):
    rows, cols = mesh.shape["row"], mesh.shape["col"]

    def shards(matrix, first, factor1, second, factor2, vectors):
        nb = first.shape[1]
        joined = jnp.concatenate([first, second], axis=1)
        panel = panel_of(joined, rows, cols)
        inner, projected = lax.psum(
            (dot(joined, joined, TN, FULL), dot(joined, vectors, TN)), "row"
        )
        cross = inner[:nb, nb:]
        top_right = -dot(dot(factor1, cross, NN, FULL), factor2, NN, FULL)
        zeros = jnp.zeros_like(factor2)
        compact = jnp.concatenate(
            [jnp.concatenate([factor1, top_right], axis=1), jnp.concatenate([zeros, factor2], axis=1)],
            axis=0,
        )
        back = vectors - dot(joined, dot(compact, projected, NN), NN)

        product = lax.psum(dot(matrix, panel, NN), "col")
        product, inner, projected = lax.optimization_barrier((product, inner, projected))
        gram = lax.psum(dot(joined, product, TN), "row")
        product_panel = panel_of(product, rows, cols)

        x1 = dot(dot(factor1, gram[:nb, :nb], TN, FULL), factor1, NN, FULL)
        key = dot(factor1, gram[nb:, :nb], ((0,), (1,)), FULL) - 0.5 * dot(x1, cross, TN, FULL)
        twist = dot(cross, key, TN, FULL)
        gram2 = gram[nb:, nb:] + twist - twist.T
        x2 = dot(dot(factor2, gram2, TN, FULL), factor2, NN, FULL)
        mixed = dot(key + 0.5 * dot(x1, cross, NN, FULL), factor2, NN, FULL)
        b = jnp.concatenate(
            [jnp.concatenate([-0.5 * x1, mixed], axis=1), jnp.concatenate([zeros, -0.5 * x2], axis=1)],
            axis=0,
        )
        skew = b - b.T
        right_top = dot(compact, product_panel, ((0,), (1,))) - dot(skew, panel, NT)
        right_low = -dot(compact, panel, NT)
        left = jnp.concatenate([joined, product], axis=1)
        right = jnp.concatenate([right_top, right_low], axis=0)
        return matrix + dot(left, right, NN), back

    in_specs = (P("row", "col"), P("row", None), P(), P("row", None), P(), P("row", "col"))
    out_specs = (P("row", "col"), P("row", "col"))
    return jax.shard_map(shards, mesh=mesh, in_specs=in_specs, out_specs=out_specs, check_vma=False)
```

time: 559 us -> 392 us (0.70); the launches traced: 549 us -> 391 us
  matrix products: 304 us -> 99.7 us
  starting transfers between devices: 0.24 us -> 27.2 us
  other arithmetic: 0 us -> 20.4 us
    dot_general x26 -> x21, matrix products: 304 us -> 99.7 us  [dot(): lax.dot_general(left, right, (dims, ((), ())), precision=precision, prefe...]
    all_gather x2 -> x0, waiting for transfers between devices: 89.3 us -> none  [the longest x1 58.9 us: shards(): lax.all_gather(first_reflector, 'row', axis=0, tiled=True)]
    ppermute x0 -> x12, waiting for transfers between devices: none -> 57 us  [the longest x8 57 us: panel_of(): part = part + lax.ppermute(part, ('row', 'col'), pairs)]
    psum x4 -> x3, waiting for transfers between devices: 129 us -> 162 us  [the longest x1 83.8 us: shards(): product = lax.psum(dot(matrix, panel, NN), 'col')]
    ppermute x0 -> x12, starting transfers between devices: none -> 26.9 us  [the longest x8 26.7 us: panel_of(): part = part + lax.ppermute(part, ('row', 'col'), pairs)]
    add x0 -> x8, other arithmetic: none -> 11.1 us  [panel_of(): part = part + lax.ppermute(part, ('row', 'col'), pairs)]
    select_n x0 -> x4, other arithmetic: none -> 8.5 us  [the longest x2 5.49 us: panel_of(): jnp.where(even, first, second)]
  transfers between devices with their start and end apart: 6 -> 15, of which waited for: 4 -> 8; matrix products, arithmetic and copies ran while one was open for 25% -> 21% of each run, Pallas kernels for 0% -> 0%
where the time goes in v1:
time: 392 us; the launch traced here: 391 us
  waiting for transfers between devices  219 us (56%)
  matrix products  99.7 us (25%)
  starting transfers between devices  27.2 us (7%)
  other arithmetic  20.4 us (5%)
  between operations  14.2 us (4%)
  local copies, waits for them, and re-layouts  10.1 us (3%)
    dot_general x21, matrix products, dot(): lax.dot_general(left, right, (dims, ((), ())), precision=precision, prefe...  99.7 us
    psum x1, waiting for transfers between devices, shards(): product = lax.psum(dot(matrix, panel, NN), 'col')  83.8 us
    ppermute x8, waiting for transfers between devices, panel_of(): part = part + lax.ppermute(part, ('row', 'col'), pairs)  57 us
    psum x1, waiting for transfers between devices, shards(): gram = lax.psum(dot(joined, product, TN), 'row')  45.9 us
    psum x1, waiting for transfers between devices, shards(): lax.psum((dot(joined, joined, TN, FULL), dot(joined, vectors, TN)), 'row')  32.3 us
    ppermute x8, starting transfers between devices, panel_of(): part = part + lax.ppermute(part, ('row', 'col'), pairs)  26.7 us
    add x8, other arithmetic, panel_of(): part = part + lax.ppermute(part, ('row', 'col'), pairs)  11.1 us
  transfers between devices with their start and end apart: 15, of which 8 were waited for; matrix products, arithmetic and copies ran while one was open for 21% of the time, Pallas kernels for 0%

profile of v1, /device:TPU:0, one launch (start us, length us, event | category | flops | bytes accessed | tf_op | source)
XLA Modules:
  0.0 390.5 jit_solution(15743474741430512661)
XLA Ops:
  7.2 1.6 copy.10
  8.9 0.3 copy.11
  9.2 0.2 fusion.21
  9.4 5.2 %collective-permute-start = (f32[1024,256]{0,1:T(8,128)S(1)}, f32[1024,256]{0,1:T(8,128)S(1)}, u32[]{:S(2)}, u32[]{:S(2)}) collective-permute-start(f32[1024,256]{0,1:T(8,128)S(1)} %get-tuple-element.13), channel_id=1, source_target_pairs={{0,8},{4,12},{9,1},{13,5},{18,26},{22,30},{27,19},{31,23}} | collective-permute-start | bytes 3145736 | tf_op jit(solution)/shard_map/ppermute | solution.py:49
  14.6 1.4 collective-permute-start.2
  16.0 21.0 %collective-permute-done = f32[1024,256]{0,1:T(8,128)S(1)} collective-permute-done((f32[1024,256]{0,1:T(8,128)S(1)}, f32[1024,256]{0,1:T(8,128)S(1)}, u32[]{:S(2)}, u32[]{:S(2)}) %collective-permute-start) | collective-permute-done | bytes 1048608 | tf_op jit(solution)/shard_map/ppermute | solution.py:49
  37.0 0.2 add.52
  37.1 1.6 collective-permute-start.1
  38.8 0.2 add.54
  38.9 4.5 %collective-permute-start.3 = (f32[1024,256]{0,1:T(8,128)S(1)}, f32[1024,256]{0,1:T(8,128)S(1)}, u32[]{:S(2)}, u32[]{:S(2)}) collective-permute-start(f32[1024,256]{0,1:T(8,128)S(1)} %add.54), channel_id=1, source_target_pairs={{0,8},{4,12},{16,24},{20,28},{9,1},{13,5},{25,17},{29,21},{18,26},... | collective-permute-start | bytes 3145736 | tf_op jit(solution)/shard_map/ppermute | solution.py:49
  43.4 17.4 %collective-permute-done.1 = f32[1024,256]{0,1:T(8,128)S(1)} collective-permute-done((f32[1024,256]{0,1:T(8,128)S(1)}, f32[1024,256]{0,1:T(8,128)S(1)}, u32[]{:S(2)}, u32[]{:S(2)}) %collective-permute-start.1) | collective-permute-done | bytes 1048608 | tf_op jit(solution)/shard_map/ppermute | solution.py:49
  60.8 0.2 add.53
  61.0 0.1 collective-permute-start.4
  61.1 3.8 collective-permute-done.3
  64.9 1.1 add.55
  66.0 2.6 fusion.23
  68.6 5.5 %fusion.22 = f32[256,1024]{1,0:T(8,128)} fusion(f32[2048,1024]{1,0:T(8,128)S(1)} %bitcast.33, f32[2048,128]{0,1:T(8,128)S(1)} %copy.11, f32[2048,128]{0,1:T(8,128)S(1)} %copy.10), kind=kOutput, calls=%fused_computation.42 | convolution fusion | flops 3221749760 | bytes 11534336 | tf_op jit(solution)/shard_map/dot_general | solution.py:11
  74.1 0.2 all-reduce.7.cloned.1.call-start
  74.3 1.3 constant_dynamic-update-slice_fusion.1
  75.7 1.3 constant_dynamic-update-slice_fusion
  77.0 3.8 fusion.15
  80.8 19.5 %convolution_bitcast_fusion = f32[2048,256]{0,1:T(8,128)} fusion(f32[2048,4096]{1,0:T(8,128)} %param.6, f32[2048,256]{0,1:T(8,128)} %get-tuple-element.9, f32[2048,256]{0,1:T(8,128)} %get-tuple-element.8), kind=kOutput, calls=%fused_computation.21 | convolution fusion | flops 12885950464 | bytes 39845888 | tf_op jit(solution)/shard_map/dot_general | solution.py:11
  100.4 0.8 copy-done.3
  101.1 0.1 copy.12
  101.2 0.1 copy.13
  101.3 32.3 %all-reduce.11.cloned.1.call-done = (f32[256,256]{1,0:T(8,128)}, f32[256,1024]{1,0:T(8,128)}) async-done(((f32[256,256]{1,0:T(8,128)}, f32[256,1024]{1,0:T(8,128)}), (f32[256,256]{1,0:T(8,128)}, f32[256,1024]{1,0:T(8,128)})) %all-reduce.11.cloned.1.call-update) | async-done | bytes 1310736 | tf_op jit(solution)/shard_map/psum | solution.py:67
  133.7 1.1 fusion.37
  134.8 0.3 convolution_negate_fusion.1
  135.1 2.9 fusion.25
  138.0 83.8 %all-reduce.7.cloned.1.call-done = f32[2048,256]{0,1:T(8,128)} async-done(((f32[2048,256]{0,1:T(8,128)}), f32[2048,256]{0,1:T(8,128)}) %all-reduce.7.cloned.1.call-update) | async-done | bytes 2097168 | tf_op jit(solution)/shard_map/psum | solution.py:79
  221.8 2.8 slice_select_fusion
  224.7 4.3 %collective-permute-start.8 = (f32[1024,256]{0,1:T(8,128)S(1)}, f32[1024,256]{0,1:T(8,128)}, u32[]{:S(2)}, u32[]{:S(2)}) collective-permute-start(f32[1024,256]{0,1:T(8,128)S(1)} %get-tuple-element.10), channel_id=1, source_target_pairs={{0,16},{4,20},{9,25},{13,29},{18,2},{22,6},{27,11},{31,15}} | collective-permute-start | bytes 3145736 | tf_op jit(solution)/shard_map/ppermute | solution.py:49
  229.0 2.4 collective-permute-start.6
  231.5 8.1 %convolution_subtract_fusion.1 = f32[2048,1024]{1,0:T(8,128)} fusion(f32[2048,1024]{1,0:T(8,128)} %param.11, f32[256,1024]{1,0:T(8,128)S(1)} %copy-done.1, f32[2048,128]{0,1:T(8,128)S(1)} %copy.11, f32[2048,128]{0,1:T(8,128)S(1)} %copy.10), kind=kOutput, calls=%fused_computation.6 | convolution fusion | flops 3223846912 | bytes 19922944 | tf_op jit(solution)/shard_map/dot_general | solution.py:11
  239.5 1.9 fusion.24
  241.5 6.2 %convolution_negate_fusion = f32[256,4096]{1,0:T(8,128)} fusion(f32[2048,256]{0,1:T(8,128)} %get-tuple-element.9, f32[2048,256]{0,1:T(8,128)} %get-tuple-element.8, f32[128,128]{0,1:T(8,128)S(1)} %copy.13, f32[128,128]{0,1:T(8,128)S(1)} %convolution_negate_fusion.1, f32[128,128]{0,1:T(8,128)S(1)} %copy.12), kind=kOutput, calls=%fused_computation.4 | convolution fusion | flops 1612972032 | bytes 8585216 | tf_op jit(solution)/shard_map/dot_general | solution.py:11
  247.7 45.9 %all-reduce.9.cloned.1.call-done = f32[256,256]{1,0:T(8,128)} async-done(((f32[256,256]{1,0:T(8,128)}), f32[256,256]{1,0:T(8,128)}) %all-reduce.9.cloned.1.call-update) | async-done | bytes 262160 | tf_op jit(solution)/shard_map/psum | solution.py:81
  293.6 1.1 fusion.30
  294.8 2.8 add.56
  297.6 3.9 collective-permute-start.7
  301.4 0.9 broadcast_multiply_fusion
  302.3 2.4 add.58
  304.7 3.5 collective-permute-start.9
  308.2 1.0 convolution_bitcast_fusion.1
  309.2 0.3 fusion.17
  309.5 0.3 fusion.33
  309.8 0.1 copy.15
  309.9 1.2 fusion.27
  311.1 10.9 %collective-permute-done.7 = f32[1024,256]{0,1:T(8,128)} collective-permute-done((f32[1024,256]{0,1:T(8,128)}, f32[1024,256]{0,1:T(8,128)}, u32[]{:S(2)}, u32[]{:S(2)}) %collective-permute-start.7) | collective-permute-done | bytes 1048608 | tf_op jit(solution)/shard_map/ppermute | solution.py:49
  322.0 1.7 add.57
  323.7 0.1 collective-permute-start.10
  323.8 1.1 fusion.16
  325.0 3.8 collective-permute-done.9
  328.8 2.7 add.59
  331.5 0.3 fusion.55
  331.8 0.3 convolution_multiply_fusion
  332.1 0.7 select_maximum_fusion
  332.8 1.8 copy.17
  334.6 4.6 %fusion.11 = f32[256,4096]{1,0:T(8,128)S(1)} fusion(f32[2048,256]{0,1:T(8,128)} %get-tuple-element.9, f32[2048,256]{0,1:T(8,128)} %get-tuple-element.8, f32[256,256]{1,0:T(8,128)} %copy.17, f32[128,128]{0,1:T(8,128)S(1)} %convolution_multiply_fusion, f32[128,128]{0,1:T(8,128)S(1)} %fusion.55, f32[128,128]{0,1:T(8,128)} %get-tuple-element.14), kind=kOutput, calls=%fused_computation.22 | convolution fusion | flops 1611988992 | bytes 8847360 | tf_op jit(solution)/shard_map/dot_general | solution.py:11
  339.2 1.3 constant_dynamic-update-slice_fusion.3
  340.5 1.3 constant_dynamic-update-slice_fusion.2
  341.8 1.7 fusion.13
  343.5 4.7 %convolution_subtract_fusion = f32[256,4096]{1,0:T(8,128)} fusion(f32[256,4096]{1,0:T(8,128)S(1)} %fusion.11, f32[2048,256]{0,1:T(8,128)S(1)} %get-tuple-element.7, f32[2048,256]{0,1:T(8,128)S(1)} %get-tuple-element.6, f32[128,128]{0,1:T(8,128)S(1)} %copy.13, f32[128,128]{0,1:T(8,128)S(1)} %convolution_negate_fusion.1, f32[128,128]{0,1:T(8,128)S(1)} %copy.12), kind=kOutput, calls=%fused_computation.5 | convolution fusion | flops 1612972032 | bytes 12779520 | tf_op jit(solution)/shard_map/dot_general | solution.py:11
  348.2 35.8 %convolution_add_fusion = f32[2048,4096]{1,0:T(8,128)} fusion(f32[2048,4096]{1,0:T(8,128)} %param.6, f32[256,4096]{1,0:T(8,128)} %convolution_negate_fusion, f32[256,4096]{1,0:T(8,128)} %convolution_subtract_fusion, f32[2048,256]{0,1:T(8,128)} %all-reduce.7.cloned.1.call-done, f32[2048,128]{0,1:T(8,128)S(1)} %copy.11, f32[2048,128]{0,1:T(8,128)S(1)} %copy.10), kind=kOutput, calls=%fused_computation | convolution fusion | flops 25782386688 | bytes 79691776 | tf_op jit(solution)/shard_map/dot_general | solution.py:11
  (36 shorter events, 0.2 us)
Async XLA Ops:
  7.2 1.7 copy-start.4
  7.2 126.5 %all-reduce.11.cloned.1.call-start = ((), (), s32[]{:S(2)}) async-start(), calls=%async_computation.2 | async-start | bytes 2621440 | tf_op jit(solution)/shard_map/psum | solution.py:67
  9.2 59.3 %slice-start = ((s8[8388608]{0:T(1024)(128)(4,1)}), s8[4194304]{0:T(1024)(128)(4,1)S(1)}, s32[]{:S(2)}) async-start(s8[8388608]{0:T(1024)(128)(4,1)} %bitcast.32), calls=%async_computation.3 | async-start | bytes 8388608
  9.4 27.5 %collective-permute-start = (f32[1024,256]{0,1:T(8,128)S(1)}, f32[1024,256]{0,1:T(8,128)S(1)}, u32[]{:S(2)}, u32[]{:S(2)}) collective-permute-start(f32[1024,256]{0,1:T(8,128)S(1)} %get-tuple-element.13), channel_id=1, source_target_pairs={{0,8},{4,12},{9,1},{13,5},{18,26},{22,30},{27,19},{31,23}} | collective-permute-start | bytes 3145736 | tf_op jit(solution)/shard_map/ppermute | solution.py:49
  14.6 24.1 %collective-permute-start.2 = (f32[1024,256]{0,1:T(8,128)S(1)}, f32[1024,256]{0,1:T(8,128)S(1)}, u32[]{:S(2)}, u32[]{:S(2)}) collective-permute-start(f32[1024,256]{0,1:T(8,128)S(1)} %get-tuple-element.12), channel_id=1, source_target_pairs={{0,16},{4,20},{9,25},{13,29},{18,2},{22,6},{27,11},{31,15}} | collective-permute-start | bytes 3145736 | tf_op jit(solution)/shard_map/ppermute | solution.py:49
  37.1 31.4 %slice-start.1 = ((s8[8388608]{0:T(1024)(128)(4,1)}), s8[4194304]{0:T(1024)(128)(4,1)S(1)}, s32[]{:S(2)}) async-start(s8[8388608]{0:T(1024)(128)(4,1)} %bitcast.32), calls=%async_computation.4 | async-start | bytes 8388608
  37.1 23.7 %collective-permute-start.1 = (f32[1024,256]{0,1:T(8,128)S(1)}, f32[1024,256]{0,1:T(8,128)S(1)}, u32[]{:S(2)}, u32[]{:S(2)}) collective-permute-start(f32[1024,256]{0,1:T(8,128)S(1)} %add.52), channel_id=1, source_target_pairs={{0,16},{4,20},{8,24},{12,28},{9,25},{13,29},{1,17},{5,21},{18,2},{... | collective-permute-start | bytes 3145736 | tf_op jit(solution)/shard_map/ppermute | solution.py:49
  38.9 25.9 %collective-permute-start.3 = (f32[1024,256]{0,1:T(8,128)S(1)}, f32[1024,256]{0,1:T(8,128)S(1)}, u32[]{:S(2)}, u32[]{:S(2)}) collective-permute-start(f32[1024,256]{0,1:T(8,128)S(1)} %add.54), channel_id=1, source_target_pairs={{0,8},{4,12},{16,24},{20,28},{9,1},{13,5},{25,17},{29,21},{18,26},... | collective-permute-start | bytes 3145736 | tf_op jit(solution)/shard_map/ppermute | solution.py:49
  61.0 13.3 %collective-permute-start.4 = (f32[1024,256]{0,1:T(8,128)S(1)}, f32[1024,256]{0,1:T(8,128)}, u32[]{:S(2)}, u32[]{:S(2)}) collective-permute-start(f32[1024,256]{0,1:T(8,128)S(1)} %add.53), channel_id=1, source_target_pairs={{0,4},{4,0},{8,12},{12,8},{16,20},{20,16},{24,28},{28,24},{1,5},{5... | collective-permute-start | bytes 3145736 | tf_op jit(solution)/shard_map/ppermute | solution.py:52
  66.0 9.7 %collective-permute-start.5 = (f32[1024,256]{0,1:T(8,128)}, f32[1024,256]{0,1:T(8,128)}, u32[]{:S(2)}, u32[]{:S(2)}) collective-permute-start(f32[1024,256]{0,1:T(8,128)} %add.55), channel_id=1, source_target_pairs={{0,4},{4,0},{8,12},{12,8},{16,20},{20,16},{24,28},{28,24},{1,5},{5... | collective-permute-start | bytes 3145736 | tf_op jit(solution)/shard_map/ppermute | solution.py:52
  74.1 147.8 %all-reduce.7.cloned.1.call-start = ((), (), s32[]{:S(2)}) async-start(), calls=%async_computation | async-start | bytes 4194304 | tf_op jit(solution)/shard_map/psum | solution.py:79
  100.3 0.8 copy-start.3
  100.3 0.9 copy-start.2
  100.3 193.3 %all-reduce.9.cloned.1.call-start = ((), (), s32[]{:S(2)}) async-start(), calls=%async_computation.1 | async-start | bytes 524288 | tf_op jit(solution)/shard_map/psum | solution.py:81
  221.8 9.6 %copy-start.1 = (f32[256,1024]{1,0:T(8,128)S(1)}, f32[256,1024]{1,0:T(8,128)}, u32[]{:S(2)}) copy-start(f32[256,1024]{1,0:T(8,128)} %fusion.25) | copy-start | bytes 3145732
  224.7 77.6 %collective-permute-start.8 = (f32[1024,256]{0,1:T(8,128)S(1)}, f32[1024,256]{0,1:T(8,128)}, u32[]{:S(2)}, u32[]{:S(2)}) collective-permute-start(f32[1024,256]{0,1:T(8,128)S(1)} %get-tuple-element.10), channel_id=1, source_target_pairs={{0,16},{4,20},{9,25},{13,29},{18,2},{22,6},{27,11},{31,15}} | collective-permute-start | bytes 3145736 | tf_op jit(solution)/shard_map/ppermute | solution.py:49
  229.0 10.5 %copy-start = (f32[2048,256]{0,1:T(8,128)S(1)}, f32[2048,256]{0,1:T(8,128)}, u32[]{:S(2)}) copy-start(f32[2048,256]{0,1:T(8,128)} %all-reduce.7.cloned.1.call-done) | copy-start | bytes 6291460
  229.0 65.7 %collective-permute-start.6 = (f32[1024,256]{0,1:T(8,128)}, f32[1024,256]{0,1:T(8,128)}, u32[]{:S(2)}, u32[]{:S(2)}) collective-permute-start(f32[1024,256]{0,1:T(8,128)} %get-tuple-element.11), channel_id=1, source_target_pairs={{0,8},{4,12},{9,1},{13,5},{18,26},{22,30},{27,19},{31,23}} | collective-permute-start | bytes 3145736 | tf_op jit(solution)/shard_map/ppermute | solution.py:49
  297.5 11.7 %copy-start.8 = (f32[256,256]{1,0:T(8,128)S(1)}, f32[256,256]{1,0:T(8,128)}, u32[]{:S(2)}) copy-start(f32[256,256]{1,0:T(8,128)} %get-tuple-element.4) | copy-start | bytes 786436
  297.6 24.5 %collective-permute-start.7 = (f32[1024,256]{0,1:T(8,128)}, f32[1024,256]{0,1:T(8,128)}, u32[]{:S(2)}, u32[]{:S(2)}) collective-permute-start(f32[1024,256]{0,1:T(8,128)} %add.56), channel_id=1, source_target_pairs={{0,16},{4,20},{8,24},{12,28},{9,25},{13,29},{1,17},{5,21},{18,2},{... | collective-permute-start | bytes 3145736 | tf_op jit(solution)/shard_map/ppermute | solution.py:49
  302.3 6.9 %copy-start.6 = (f32[128,128]{0,1:T(8,128)}, f32[128,128]{0,1:T(8,128)S(1)}, u32[]{:S(2)}) copy-start(f32[128,128]{0,1:T(8,128)S(1)} %get-tuple-element.15) | copy-start | bytes 196612
  304.7 24.1 %collective-permute-start.9 = (f32[1024,256]{0,1:T(8,128)}, f32[1024,256]{0,1:T(8,128)}, u32[]{:S(2)}, u32[]{:S(2)}) collective-permute-start(f32[1024,256]{0,1:T(8,128)} %add.58), channel_id=1, source_target_pairs={{0,8},{4,12},{16,24},{20,28},{9,1},{13,5},{25,17},{29,21},{18,26},... | collective-permute-start | bytes 3145736 | tf_op jit(solution)/shard_map/ppermute | solution.py:49
  309.9 13.9 %copy-start.7 = (f32[128,128]{0,1:T(8,128)S(1)}, f32[128,128]{0,1:T(8,128)}, u32[]{:S(2)}) copy-start(f32[128,128]{0,1:T(8,128)} %copy-done.6) | copy-start | bytes 196612
  323.7 8.4 %copy-start.5 = (f32[128,128]{0,1:T(8,128)S(1)}, f32[128,128]{0,1:T(8,128)}, u32[]{:S(2)}) copy-start(f32[128,128]{0,1:T(8,128)} %get-tuple-element.14) | copy-start | bytes 196612
  323.7 15.5 %collective-permute-start.10 = (f32[1024,256]{0,1:T(8,128)S(1)}, f32[1024,256]{0,1:T(8,128)}, u32[]{:S(2)}, u32[]{:S(2)}) collective-permute-start(f32[1024,256]{0,1:T(8,128)S(1)} %add.57), channel_id=1, source_target_pairs={{0,4},{4,0},{8,12},{12,8},{16,20},{20,16},{24,28},{28,24},{1,5},{5... | collective-permute-start | bytes 3145736 | tf_op jit(solution)/shard_map/ppermute | solution.py:52
  331.5 9.0 %collective-permute-start.11 = (f32[1024,256]{0,1:T(8,128)}, f32[1024,256]{0,1:T(8,128)}, u32[]{:S(2)}, u32[]{:S(2)}) collective-permute-start(f32[1024,256]{0,1:T(8,128)} %add.59), channel_id=1, source_target_pairs={{0,4},{4,0},{8,12},{12,8},{16,20},{20,16},{24,28},{28,24},{1,5},{5... | collective-permute-start | bytes 3145736 | tf_op jit(solution)/shard_map/ppermute | solution.py:52
Sparse Core Ops, SparseCore 0:
  74.2 59.4 all-reduce.10
  136.6 85.1 all-reduce.6
  241.6 51.9 all-reduce.8
